TPU v7x, 512 devices: a whole 4x8x8 slice. The times are simulated.
512 devices in a mesh: ctx: 64 (over z, y), mp: 8 (over x, core).
Axes of the slice: x: 4, y: 8, z: 8, core: 2. Of those that a mesh axis runs over, the one named last changes fastest.
Arguments:
- seq_in: bfloat16 [8192, 8192], P('ctx', 'mp'), may hold values from -6 to 6
- gate_in: bfloat16 [8192, 8192], P('ctx', 'mp'), may hold values from -6 to 6
- upstream: bfloat16 [8192, 8192], P('ctx', 'mp'), may hold values from -6 to 6
- forget_flags: int32 [8192], P('ctx'), may hold values 0 or 1
- conv_weight: float32 [4, 8192], P(None, 'mp'), may hold values from -3 to 3
- conv_bias: float32 [8192], P('mp'), may hold values from -3 to 3
- proj_weight: bfloat16 [8192, 544], P(('mp', 'ctx')), may hold values from -0.0625 to 0.0625
- dt_weight: bfloat16 [512, 8192], P('ctx', 'mp'), may hold values from -0.25 to 0.25
- dt_bias: float32 [8192], P('mp'), may hold values from -10 to -3
- a_log: float32 [16, 8192], P(None, 'mp'), may hold values from 0 to 2.77
- skip_gain: float32 [8192], P('mp'), may hold values from 0.5 to 1.5
Outputs:
- grad_seq: bfloat16 [8192, 8192], P('ctx', 'mp')
- grad_gate: bfloat16 [8192, 8192], P('ctx', 'mp')
- grad_dt_weight: float32 [512, 8192], P('ctx', 'mp')
- grad_conv_weight: float32 [4, 8192], P(None, ('mp', 'ctx'))
- grad_conv_bias: float32 [8192], P(('mp', 'ctx'))
- grad_dt_bias: float32 [8192], P(('mp', 'ctx'))
- grad_a_log: float32 [16, 8192], P(None, ('mp', 'ctx'))
- grad_skip: float32 [8192], P(('mp', 'ctx'))
All inputs are finite; a program needn't handle non-finite values. No bound on the sum of `forget_flags` on one device may be relied on, other than what follows from the above.
Results may differ from a plain program's by a relative error of at most 0.017.
Values may be sent and summed in bfloat16 or wider, within the bound.
A program may use at most 64 MiB of HBM per device.

v0:
```python
import jax
import jax.numpy as jnp
from jax import lax
from jax.sharding import PartitionSpec as P

STATE = 16
RANK = 512
CONV = 4


def shifted(block, axis, distance):
    devices = range(lax.axis_size(axis))
    route = [(i - distance, i) for i in devices if i - distance in devices]
    return lax.ppermute(block, axis, route)


def prefix(x, axis, combine, identity, reverse):
    count, mine = (lax.axis_size(axis), lax.axis_index(axis))
    everything = jax.tree.map(lambda part: lax.all_gather(part, axis), x)
    start = jax.tree.map(
        lambda part, zero: jnp.broadcast_to(jnp.asarray(zero, part.dtype), part.shape), x, identity
    )

    def step(k, before):
        at = count - 1 - k if reverse else k
        reached = at > mine if reverse else at < mine
        new = combine(before, jax.tree.map(lambda part: part[at], everything))
        return jax.tree.map(lambda a, b: jnp.where(reached, a, b), new, before)

    return lax.fori_loop(0, count, step, start)


def to_blocks(arrays):
    return tuple((a.reshape((a.shape[0] // 16, 16) + a.shape[1:]) for a in arrays))


def block_closed(carry, inputs):
    state, a_matrix = carry
    act_blk, step_blk, b_blk, c_blk = inputs
    rows = step_blk.shape[0]
    cumul = jnp.cumsum(step_blk[:, None, :] * a_matrix[None], axis=0)
    later_rows = lax.broadcasted_iota(jnp.int32, (rows, rows), 0)
    early_rows = lax.broadcasted_iota(jnp.int32, (rows, rows), 1)
    lower = (later_rows >= early_rows)[:, :, None, None]
    gaps = jnp.where(lower, cumul[:, None] - cumul[None, :], 0.0)
    weights = jnp.where(lower, jnp.exp(gaps), 0.0)
    inflow = b_blk[:, :, None] * (step_blk * act_blk)[:, None, :]
    states = jnp.exp(cumul) * state[None] + jnp.sum(weights * inflow[None], axis=1)
    outputs = jnp.sum(c_blk[:, :, None] * states, axis=1)
    return ((states[-1], a_matrix), outputs)


def scan_tokens(act_full, step_size, b_matrix, c_matrix, log_rates, skip):
    a_matrix = -jnp.exp(log_rates)
    length = act_full.shape[0]
    start_state = jnp.zeros(log_rates.shape, jnp.float32)
    carry, outputs = lax.scan(
        jax.checkpoint(block_closed),
        (start_state, a_matrix),
        to_blocks((act_full, step_size, b_matrix, c_matrix)),
    )
    return (outputs.reshape(length, -1) + skip[None, :] * act_full, carry[0])


def carry_block(carry, inputs):
    state, a_matrix = carry
    step_blk, c_blk = inputs
    cumul = jnp.cumsum(step_blk[:, None, :] * a_matrix[None], axis=0)
    states = jnp.exp(cumul) * state[None]
    return ((states[-1], a_matrix), jnp.sum(c_blk[:, :, None] * states, axis=1))


def carry_in(step_size, c_matrix, log_rates, state_in):
    a_matrix = -jnp.exp(log_rates)
    length = step_size.shape[0]
    carry, outputs = lax.scan(
        jax.checkpoint(carry_block), (state_in, a_matrix), to_blocks((step_size, c_matrix))
    )
    return (outputs.reshape(length, -1), carry[0])


def compose(earlier, later):
    return (earlier[0] * later[0], later[0] * earlier[1] + later[1])


def body(
    seq_in,
    gate_in,
    upstream,
    forget_flags,
    conv_weight,
    conv_bias,
    proj_weight,
    dt_weight,
    dt_bias,
    a_log,
    skip_gain,
):
    length = seq_in.shape[0]
    rim_rows = CONV - 1
    from_left = shifted(seq_in[length - rim_rows :], "ctx", 1)
    padded = jnp.concatenate([from_left, seq_in], axis=0)
    pre_act = jnp.zeros(seq_in.shape, jnp.float32) + conv_bias[None, :]
    for k in range(CONV):
        pre_act = pre_act + conv_weight[k][None, :] * padded[k : k + length]
    act_half = jax.nn.silu(pre_act).astype(jnp.bfloat16)
    rows_proj, rows_dt = (
        lax.all_gather(proj_weight, "ctx", axis=0, tiled=True),
        lax.all_gather(dt_weight, "ctx", axis=0, tiled=True),
    )
    partial_proj = jnp.dot(act_half, rows_proj, preferred_element_type=jnp.float32)
    projected = lax.psum(partial_proj, "mp")
    dt_low = projected[:, :RANK].astype(jnp.bfloat16)
    b_matrix = projected[:, RANK : RANK + STATE]
    c_matrix = projected[:, RANK + STATE :]
    dt_pre = jnp.dot(dt_low, rows_dt, preferred_element_type=jnp.float32) + dt_bias[None, :]
    step_size = jax.nn.softplus(dt_pre)
    a_matrix = -jnp.exp(a_log)
    act_full = act_half.astype(jnp.float32)
    (mixed_local, state_end), pull_local = jax.vjp(
        scan_tokens, act_full, step_size, b_matrix, c_matrix, a_log, skip_gain
    )
    zeros_state = jnp.zeros_like(state_end)
    step_totals = jnp.sum(step_size, axis=0)
    decays = jnp.exp(a_matrix * step_totals[None, :])
    state_in = prefix(
        (decays, state_end), "ctx", compose, (jnp.ones_like(decays), zeros_state), False
    )[1]
    (mixed_carry, unused_end), pull_carry = jax.vjp(carry_in, step_size, c_matrix, a_log, state_in)
    mixed = mixed_local + mixed_carry
    flag_values = forget_flags.astype(jnp.float32)
    grad_out = -flag_values[:, None] * upstream.astype(jnp.float32)
    gate_full = gate_in.astype(jnp.float32)
    gate_sigmoid = jax.nn.sigmoid(gate_full)
    grad_mixed = grad_out * (gate_full * gate_sigmoid)
    grad_gate = (
        grad_out * mixed * (gate_sigmoid * (1.0 + gate_full * (1.0 - gate_sigmoid)))
    ).astype(jnp.bfloat16)
    local_adjoint = pull_carry((grad_mixed, zeros_state))[3]
    adjoint_out = prefix(
        (decays, local_adjoint), "ctx", compose, (jnp.ones_like(decays), zeros_state), True
    )[1]
    grad_act_scan, grad_step, grad_bmat, grad_cmat, grad_rate, grad_skip = pull_local(
        (grad_mixed, adjoint_out)
    )
    extra_step, extra_cmat, extra_rate, unused_in = pull_carry((grad_mixed, adjoint_out))
    grad_step = grad_step + extra_step
    grad_cmat = grad_cmat + extra_cmat
    grad_rate = grad_rate + extra_rate
    grad_pre = grad_step * jax.nn.sigmoid(dt_pre)
    grad_pre_half = grad_pre.astype(jnp.bfloat16)
    grad_dtw = lax.dot_general(
        dt_low, grad_pre_half, (((0,), (0,)), ((), ())), preferred_element_type=jnp.float32
    )
    grad_low = lax.dot_general(
        grad_pre_half, rows_dt, (((1,), (1,)), ((), ())), preferred_element_type=jnp.float32
    )
    grad_proj = lax.psum(
        jnp.concatenate([grad_low, grad_bmat, grad_cmat], axis=1).astype(jnp.bfloat16), "mp"
    )
    grad_from_proj = lax.dot_general(
        grad_proj, rows_proj, (((1,), (1,)), ((), ())), preferred_element_type=jnp.float32
    )
    act_sigmoid = jax.nn.sigmoid(pre_act)
    grad_pre_act = (grad_act_scan + grad_from_proj) * (
        act_sigmoid * (1.0 + pre_act * (1.0 - act_sigmoid))
    )
    from_next = shifted(grad_pre_act[:rim_rows], "ctx", -1)
    grad_padded = jnp.concatenate([grad_pre_act, from_next], axis=0)
    grad_seq = jnp.zeros(seq_in.shape, jnp.float32)
    for k in range(CONV):
        grad_seq = (
            grad_seq + conv_weight[k][None, :] * grad_padded[rim_rows - k : rim_rows - k + length]
        )
    grad_conv_w = jnp.stack(
        [jnp.sum(grad_pre_act * padded[k : k + length], axis=0) for k in range(CONV)]
    )
    grad_conv_b = jnp.sum(grad_pre_act, axis=0)
    grad_dt_b = jnp.sum(grad_pre, axis=0)
    summed_grads = (
        lax.psum_scatter(grad_dtw, "ctx", scatter_dimension=0, tiled=True),
        lax.psum_scatter(grad_conv_w, "ctx", scatter_dimension=1, tiled=True),
        lax.psum_scatter(grad_conv_b, "ctx", scatter_dimension=0, tiled=True),
        lax.psum_scatter(grad_dt_b, "ctx", scatter_dimension=0, tiled=True),
        lax.psum_scatter(grad_rate, "ctx", scatter_dimension=1, tiled=True),
        lax.psum_scatter(grad_skip, "ctx", scatter_dimension=0, tiled=True),
    )
    return (grad_seq.astype(jnp.bfloat16), grad_gate) + tuple(summed_grads)


def solution(mesh):
    return jax.shard_map(
        body,
        mesh=mesh,
        in_specs=(
            P("ctx", "mp"),
            P("ctx", "mp"),
            P("ctx", "mp"),
            P("ctx"),
            P(None, "mp"),
            P("mp"),
            P(("mp", "ctx"), None),
            P("ctx", "mp"),
            P("mp"),
            P(None, "mp"),
            P("mp"),
        ),
        out_specs=(
            P("ctx", "mp"),
            P("ctx", "mp"),
            P("ctx", "mp"),
            P(None, ("mp", "ctx")),
            P(("mp", "ctx")),
            P(("mp", "ctx")),
            P(None, ("mp", "ctx")),
            P(("mp", "ctx")),
        ),
        check_vma=False,
    )
```

profile of v0, /device:TPU:6, one launch (start us, length us, event | category | flops | bytes accessed | tf_op | source)
XLA Modules:
  0.0 1251.3 jit_solution(16375797547710604420)
XLA Ops:
  8.7 3.5 collective-permute-start
  13.8 2.7 multiply_reduce_fusion.15
  16.4 81.7 %all-gather.9.cloned.1.call-done = bf16[1024,544]{1,0:T(8,128)(2,1)} async-done(((bf16[16,544]{1,0:T(8,128)(2,1)}), bf16[1024,544]{1,0:T(8,128)(2,1)}) %all-gather.9.cloned.1.call-update) | async-done | bytes 1114128 | tf_op jit(solution)/shard_map/all_gather | solution.py:108
  98.2 2.7 fusion.82
  101.8 63.4 %all-reduce.15.cloned.1.call-done = f32[128,544]{0,1:T(8,128)} async-done(((f32[128,544]{0,1:T(8,128)}), f32[128,544]{0,1:T(8,128)}) %all-reduce.15.cloned.1.call-update) | async-done | bytes 278544 | tf_op jit(solution)/shard_map/psum | solution.py:112
  167.4 85.5 %all-gather.11.cloned.1.call-done = bf16[512,1024]{1,0:T(8,128)(2,1)} async-done(((bf16[8,1024]{1,0:T(8,128)(2,1)}), bf16[512,1024]{1,0:T(8,128)(2,1)}) %all-gather.11.cloned.1.call-update) | async-done | bytes 1048592 | tf_op jit(solution)/shard_map/all_gather | solution.py:109
  252.9 2.7 compare_select_fusion
  256.4 59.0 %while.128 = (s32[]{:T(128)}, f32[16,1024]{1,0:T(8,128)S(1)}, f32[8,16,1024]{2,1,0:T(8,128)S(1)}, f32[8,16,1024]{2,1,0:T(8,128)S(1)}, f32[8,16,1024]{2,1,0:T(8,1...) while((s32[]{:T(128)}, f32[16,1024]{1,0:T(8,128)S(1)}, ...), condition=%wide.region_6.7_spmd.clone.clone, body=%wide.region_2.6_spmd.clone.clone.sunk | while | flops 26214400 | bytes 9574793 | solution.py:57
  257.6 5.7 multiply_reduce_fusion.25
  265.0 5.7 multiply_reduce_fusion.25
  272.4 5.7 multiply_reduce_fusion.25
  279.8 5.7 multiply_reduce_fusion.25
  287.1 5.7 multiply_reduce_fusion.25
  294.5 5.7 multiply_reduce_fusion.25
  301.9 5.7 multiply_reduce_fusion.25
  309.2 5.7 multiply_reduce_fusion.25
  316.7 83.6 %all-gather.15.cloned.1.call-done = f32[1024,1024]{1,0:T(8,128)} async-done(((f32[16,1024]{1,0:T(8,128)}), f32[1024,1024]{1,0:T(8,128)}) %all-gather.15.cloned.1.call-update) | async-done | bytes 4194320 | tf_op jit(solution)/shard_map/all_gather | solution.py:19
  400.3 87.8 %all-gather.13.cloned.1.call-done = f32[1024,1024]{1,0:T(8,128)} async-done(((f32[16,1024]{1,0:T(8,128)}), f32[1024,1024]{1,0:T(8,128)}) %all-gather.13.cloned.1.call-update) | async-done | bytes 4194320 | tf_op jit(solution)/shard_map/all_gather | solution.py:19
  488.1 59.9 %while.129 = (s32[]{:T(128)}, f32[16,1024]{1,0:T(8,128)S(1)}, s32[]{:T(128)}, f32[64,16,1024]{2,1,0:T(8,128)}, f32[64,16,1024]{2,1,0:T(8,128)}, /*index=5*/s32[]{:T(128)}, s32[]{:T(128)}) while((s32[]{:T(128)}, f32[16,1024]{1,0:T(8,128)S(1)}, s32[]{:T(128)}, f32[64,16,1024]{2,1,0:T(8,128)}, f32[64,16,1024]{2,1,0:T(8,128)}, ...), condition=%wide.region_8.9_spmd.clone, body=%wide.region_7.8_spmd.clone.sunk | while | flops 65540 | bytes 262245 | solution.py:30
  549.1 14.5 %while.126 = (s32[]{:T(128)}, f32[16,1024]{1,0:T(8,128)S(1)}, f32[8,16,1024]{2,1,0:T(8,128)S(1)}, f32[8,16,1024]{2,1,0:T(8,128)}, f32[8,16,1024]{2,1,0:T(8,128)S...) while((s32[]{:T(128)}, f32[16,1024]{1,0:T(8,128)S(1)}, ...), condition=%wide.region_12.13_spmd, body=%wide.region_9.12_spmd.sunk | while | flops 4964354 | bytes 1969769 | solution.py:76
  563.6 8.2 while.127
  573.4 83.1 %all-gather.17.cloned.1.call-done = f32[1024,1024]{1,0:T(8,128)} async-done(((f32[16,1024]{1,0:T(8,128)}), f32[1024,1024]{1,0:T(8,128)}) %all-gather.17.cloned.1.call-update) | async-done | bytes 4194320 | tf_op jit(solution)/shard_map/all_gather | solution.py:19
  656.5 60.4 %while.130 = (s32[]{:T(128)}, f32[16,1024]{1,0:T(8,128)S(1)}, s32[]{:T(128)}, f32[64,16,1024]{2,1,0:T(8,128)}, f32[64,16,1024]{2,1,0:T(8,128)}, /*index=5*/s32[]{:T(128)}, s32[]{:T(128)}, s32[]{:T(128)}, s32[]{:T(128)}) while((s32[]{:T(128)}, f32[16,1024]{1,0:T(8,128)S(1)}, s32[]{:T(128)}, f32[64,16,1024]{2,1,0:T(8,128)}, ...), condition=%wide.region_18.19_spmd.clone, body=%wide.region_17.18_spmd.clone.sunk | while | flops 65544 | bytes 262307 | solution.py:30
  659.3 0.9 fusion.103
  660.2 0.9 fusion.103
  663.1 0.9 fusion.103
  664.0 0.9 fusion.103
  665.0 0.9 fusion.103
  667.8 0.9 fusion.103
  668.7 0.9 fusion.103
  716.9 22.7 %while.132 = (s32[]{:T(128)}, f32[16,1024]{1,0:T(8,128)S(1)}, f32[16,1024]{1,0:T(8,128)S(1)}, f32[8,16,1024]{2,1,0:T(8,128)S(1)}, f32[8,16,16]{2,1,0:T(8,128)S(1...) while((s32[]{:T(128)}, f32[16,1024]{1,0:T(8,128)S(1)}, ...), condition=%wide.region_40.41_spmd.clone, body=%wide.region_33.40_spmd.clone.sunk | while | flops 12041988 | bytes 4084903 | solution.py:76
  742.0 138.3 %while.131 = (s32[]{:T(128)}, f32[16,1024]{1,0:T(8,128)S(1)}, f32[16,1024]{1,0:T(8,128)S(1)}, f32[8,16,1024]{2,1,0:T(8,128)}, f32[8,16,1024]{2,1,0:T(8,128)}, /*...) while((s32[]{:T(128)}, f32[16,1024]{1,0:T(8,128)S(1)}, ...), condition=%wide.region_32.33_spmd.clone, body=%wide.region_19.32_spmd.clone.sunk | while | flops 68452096 | bytes 19686096 | solution.py:57
  742.0 0.9 dynamic-slice_bitcast_fusion.43
  745.2 10.7 fusion.106
  756.2 0.9 multiply_reduce_fusion.28
  762.5 10.7 fusion.106
  773.5 0.9 multiply_reduce_fusion.28
  779.8 10.7 fusion.106
  790.7 0.9 multiply_reduce_fusion.28
  797.1 10.7 fusion.106
  808.0 0.9 multiply_reduce_fusion.28
  814.3 10.7 fusion.106
  825.3 0.9 multiply_reduce_fusion.28
  831.6 10.7 fusion.106
  842.6 0.9 multiply_reduce_fusion.28
  848.9 10.7 fusion.106
  859.8 0.9 multiply_reduce_fusion.28
  866.1 10.7 fusion.106
  877.1 0.9 multiply_reduce_fusion.28
  880.3 1.3 add.253
  881.7 1.8 fusion.78
  884.9 1.5 pad_maximum_fusion.2
  886.5 1.7 fusion.73
  888.3 1.5 add_multiply_fusion
  889.8 2.6 fusion.68
  892.4 57.6 %all-reduce.17.cloned.1.call-done = bf16[128,544]{1,0:T(8,128)(2,1)} async-done(((bf16[128,544]{1,0:T(8,128)(2,1)}), bf16[128,544]{1,0:T(8,128)(2,1)}) %all-reduce.17.cloned.1.call-update) | async-done | bytes 139280 | tf_op jit(solution)/shard_map/psum | solution.py:158
  950.1 1.9 fusion.44
  952.0 1.3 collective-permute-start.1
  953.3 1.3 dynamic-slice
  955.9 1.8 collective-permute-done.1
  957.6 1.2 fusion.57
  958.9 280.4 %all-reduce.9 = (f32[4,1024]{1,0:T(4,128)S(1)}, f32[1024]{0:T(1024)S(1)}, f32[1024]{0:T(1024)S(1)}, f32[1024]{0:T(1024)S(1)}) all-reduce(f32[4,1024]{1,0:T(4,128)S(1)} %pad_maximum_fusion.3, f32[1024]{0:T(1024)S(1)} %get-tuple-element.1399, f32[1024]{0:T(1024)S(1)} %copy-done.25, ...), channel_id=6, replica_groups=mesh['ctx'=64,'mp'=8] {'ctx'}, use_global_device_ids=true, to_apply=%region_47.48.clone | all-reduce | flops 7168 | bytes 57344
  1241.7 1.4 constant_dynamic-slice_fusion
  1243.1 1.4 constant_dynamic-slice_fusion.2
  (608 shorter events, 228.8 us)
Async XLA Ops:
  7.2 245.7 %copy-start.26 = (f32[1024]{0:T(1024)S(1)}, f32[1024]{0:T(1024)}, u32[]{:S(2)}) copy-start(f32[1024]{0:T(1024)} %param.33) | copy-start | bytes 12292
  7.2 248.4 %copy-start.12 = (f32[16,1024]{1,0:T(8,128)S(1)}, f32[16,1024]{1,0:T(8,128)}, u32[]{:S(2)}) copy-start(f32[16,1024]{1,0:T(8,128)} %param.34) | copy-start | bytes 196612
  7.2 91.0 %all-gather.9.cloned.1.call-start = ((), (), s32[]{:S(2)}) async-start(), calls=%async_computation | async-start | bytes 1331200 | tf_op jit(solution)/shard_map/all_gather | solution.py:108
  7.9 157.3 %all-reduce.15.cloned.1.call-start = ((), (), s32[]{:S(2)}) async-start(), calls=%async_computation.1 | async-start | bytes 557056 | tf_op jit(solution)/shard_map/psum | solution.py:112
  8.7 5.1 collective-permute-start
  13.1 88.6 %copy-start.14 = (f32[1,1024]{1,0:T(1,128)}, f32[1,1024]{1,0:T(1,128)S(1)}, u32[]{:S(2)}) copy-start(f32[1,1024]{1,0:T(1,128)S(1)} %get-tuple-element.1561) | copy-start | bytes 12292
  13.1 88.6 %copy-start.16 = (f32[1,1024]{1,0:T(1,128)}, f32[1,1024]{1,0:T(1,128)S(1)}, u32[]{:S(2)}) copy-start(f32[1,1024]{1,0:T(1,128)S(1)} %get-tuple-element.1562) | copy-start | bytes 12292
  13.1 88.6 %copy-start.18 = (f32[1,1024]{1,0:T(1,128)}, f32[1,1024]{1,0:T(1,128)S(1)}, u32[]{:S(2)}) copy-start(f32[1,1024]{1,0:T(1,128)S(1)} %get-tuple-element.1563) | copy-start | bytes 12292
  13.1 88.6 %copy-start.20 = (f32[1,1024]{1,0:T(1,128)}, f32[1,1024]{1,0:T(1,128)S(1)}, u32[]{:S(2)}) copy-start(f32[1,1024]{1,0:T(1,128)S(1)} %get-tuple-element.1564) | copy-start | bytes 12292
  13.8 241.8 %copy-start.28 = (f32[128]{0:T(128)}, f32[128]{0:T(128)S(1)}, u32[]{:S(2)}) copy-start(f32[128]{0:T(128)S(1)} %convert_negate_fusion.1) | copy-start | bytes 1540
  13.8 87.9 %copy-start.22 = (bf16[3,1024]{1,0:T(4,128)(2,1)}, bf16[3,1024]{1,0:T(4,128)(2,1)S(1)}, u32[]{:S(2)}) copy-start(bf16[3,1024]{1,0:T(4,128)(2,1)S(1)} %collective-permute-done) | copy-start | bytes 18436
  100.9 152.0 %all-gather.11.cloned.1.call-start = ((), (), s32[]{:S(2)}) async-start(), calls=%async_computation.2 | async-start | bytes 1064960 | tf_op jit(solution)/shard_map/all_gather | solution.py:109
  101.6 298.7 %all-gather.15.cloned.1.call-start = ((), (), s32[]{:S(2)}) async-start(), calls=%async_computation.5 | async-start | bytes 4259840 | tf_op jit(solution)/shard_map/all_gather | solution.py:19
  315.4 0.6 copy-start
  315.4 232.7 %copy-start.7 = (f32[8,16,1024]{2,1,0:T(8,128)}, f32[8,16,1024]{2,1,0:T(8,128)S(1)}, u32[]{:S(2)}) copy-start(f32[8,16,1024]{2,1,0:T(8,128)S(1)} %get-tuple-element.2193) | copy-start | bytes 1572868
  315.4 232.7 %copy-start.8 = (f32[8,16,1024]{2,1,0:T(8,128)}, f32[8,16,1024]{2,1,0:T(8,128)S(1)}, u32[]{:S(2)}) copy-start(f32[8,16,1024]{2,1,0:T(8,128)S(1)} %get-tuple-element.2194) | copy-start | bytes 1572868
  315.4 232.7 %copy-start.4 = (f32[8,16,1024]{2,1,0:T(8,128)}, f32[8,16,1024]{2,1,0:T(8,128)S(1)}, u32[]{:S(2)}) copy-start(f32[8,16,1024]{2,1,0:T(8,128)S(1)} %get-tuple-element.1049) | copy-start | bytes 1572868
  316.0 172.1 %all-gather.13.cloned.1.call-start = ((), (), s32[]{:S(2)}) async-start(), calls=%async_computation.4 | async-start | bytes 4259840 | tf_op jit(solution)/shard_map/all_gather | solution.py:19
  316.6 339.8 %all-gather.17.cloned.1.call-start = ((), (), s32[]{:S(2)}) async-start(), calls=%async_computation.6 | async-start | bytes 4259840 | tf_op jit(solution)/shard_map/all_gather | solution.py:19
  563.6 153.3 %copy-start.5 = (f32[8,16,1024]{2,1,0:T(8,128)}, f32[8,16,1024]{2,1,0:T(8,128)S(1)}, u32[]{:S(2)}) copy-start(f32[8,16,1024]{2,1,0:T(8,128)S(1)} %get-tuple-element.1050) | copy-start | bytes 1572868
  571.8 0.6 copy-start.2
  572.5 377.5 %all-reduce.17.cloned.1.call-start = ((), (), s32[]{:S(2)}) async-start(), calls=%async_computation.3 | async-start | bytes 327680 | tf_op jit(solution)/shard_map/psum | solution.py:158
  739.6 2.4 copy-start.6
  739.6 2.4 copy-start.13
  742.0 142.3 %copy-start.1 = (bf16[512,1024]{1,0:T(8,128)(2,1)S(1)}, bf16[512,1024]{1,0:T(8,128)(2,1)}, u32[]{:S(2)}) copy-start(bf16[512,1024]{1,0:T(8,128)(2,1)} %all-gather.11.cloned.1.call-done) | copy-start | bytes 3145732
  880.3 6.2 copy-start.11
  881.6 8.1 copy-start.3
  886.4 63.6 %copy-start.9 = (bf16[1024,544]{1,0:T(8,128)(2,1)S(1)}, bf16[1024,544]{1,0:T(8,128)(2,1)}, u32[]{:S(2)}) copy-start(bf16[1024,544]{1,0:T(8,128)(2,1)} %all-gather.9.cloned.1.call-done) | copy-start | bytes 3342340
  886.4 63.6 %copy-start.10 = (bf16[128,1024]{1,0:T(8,128)(2,1)S(1)}, bf16[128,1024]{1,0:T(8,128)(2,1)}, u32[]{:S(2)}) copy-start(bf16[128,1024]{1,0:T(8,128)(2,1)} %param.25) | copy-start | bytes 786436
  886.4 355.2 %all-reduce.19.cloned.1.call-start = ((), (), s32[]{:S(2)}) async-start(), calls=%async_computation.7 | async-start | bytes 4325376
  888.2 61.8 %copy-start.15 = (f32[1,1024]{1,0:T(1,128)S(1)}, f32[1,1024]{1,0:T(1,128)}, u32[]{:S(2)}) copy-start(f32[1,1024]{1,0:T(1,128)} %copy-done.14) | copy-start | bytes 12292
  888.2 61.8 %copy-start.17 = (f32[1,1024]{1,0:T(1,128)S(1)}, f32[1,1024]{1,0:T(1,128)}, u32[]{:S(2)}) copy-start(f32[1,1024]{1,0:T(1,128)} %copy-done.16) | copy-start | bytes 12292
  888.2 61.8 %copy-start.19 = (f32[1,1024]{1,0:T(1,128)S(1)}, f32[1,1024]{1,0:T(1,128)}, u32[]{:S(2)}) copy-start(f32[1,1024]{1,0:T(1,128)} %copy-done.18) | copy-start | bytes 12292
  888.2 61.8 %copy-start.21 = (f32[1,1024]{1,0:T(1,128)S(1)}, f32[1,1024]{1,0:T(1,128)}, u32[]{:S(2)}) copy-start(f32[1,1024]{1,0:T(1,128)} %copy-done.20) | copy-start | bytes 12292
  888.2 61.8 %copy-start.23 = (bf16[3,1024]{1,0:T(4,128)(2,1)S(1)}, bf16[3,1024]{1,0:T(4,128)(2,1)}, u32[]{:S(2)}) copy-start(bf16[3,1024]{1,0:T(4,128)(2,1)} %copy-done.22) | copy-start | bytes 18436
  888.3 61.8 %copy-start.27 = (f32[1024]{0:T(1024)S(1)}, f32[1024]{0:T(1024)}, u32[]{:S(2)}) copy-start(f32[1024]{0:T(1024)} %param.30) | copy-start | bytes 12292
  892.4 66.5 %copy-start.24 = (f32[1024]{0:T(1024)S(1)}, f32[1024]{0:T(1024)}, u32[]{:S(2)}) copy-start(f32[1024]{0:T(1024)} %get-tuple-element.1526) | copy-start | bytes 12292
  892.4 66.5 %copy-start.25 = (f32[1024]{0:T(1024)S(1)}, f32[1024]{0:T(1024)}, u32[]{:S(2)}) copy-start(f32[1024]{0:T(1024)} %get-tuple-element.1529) | copy-start | bytes 12292
  952.0 5.6 collective-permute-start.1
Sparse Core Ops, SparseCore 0:
  11.1 87.0 all-gather.8
  101.0 64.1 all-reduce.14
  168.7 84.1 all-gather.10
  316.2 84.1 all-gather.14
  404.3 83.8 all-gather.12
  572.6 83.8 all-gather.16
  886.5 63.4 all-reduce.16
  953.5 165.4 all-reduce.18
where the time goes:
time: 1260 us; the launch traced here: 1250 us
  waiting for transfers between devices  547 us (43%)
  other arithmetic  308 us (24%)
  blocking collectives  280 us (22%)
  local copies, waits for them, and re-layouts  80.2 us (6%)
  between operations  16 us (1%)
    unnamed x1, blocking collectives  280 us
    all_gather x3, waiting for transfers between devices, prefix(): everything = jax.tree.map(lambda part: lax.all_gather(part, axis), x)  255 us
    select_n x128, other arithmetic, step(): return jax.tree.map(lambda a, b: jnp.where(reached, a, b), new, before)  117 us
    all_gather x1, waiting for transfers between devices, body(): lax.all_gather(dt_weight, 'ctx', axis=0, tiled=True)  85.5 us
    reduce_sum x8, other arithmetic, block_closed(): gaps = jnp.where(lower, cumul[:, None] - cumul[None, :], 0.0)  85.3 us
    all_gather x1, waiting for transfers between devices, body(): lax.all_gather(proj_weight, 'ctx', axis=0, tiled=True)  81.7 us
    psum x1, waiting for transfers between devices, body(): projected = lax.psum(partial_proj, 'mp')  63.4 us
    psum x1, waiting for transfers between devices, body(): lax.psum(jnp.concatenate([grad_low, grad_bmat, grad_cmat], axis=1).astype...  57.6 us
  transfers between devices with their start and end apart: 10, of which 8 were waited for; matrix products, arithmetic and copies ran while one was open for 2% of the time, Pallas kernels for 0%

commit v1 on v0

--- a/solution.py
+++ b/solution.py
@@ -155,8 +155,11 @@
     grad_low = lax.dot_general(
         grad_pre_half, rows_dt, (((1,), (1,)), ((), ())), preferred_element_type=jnp.float32
     )
-    grad_proj = lax.psum(
-        jnp.concatenate([grad_low, grad_bmat, grad_cmat], axis=1).astype(jnp.bfloat16), "mp"
+    grad_proj = jnp.sum(
+        lax.all_gather(
+            jnp.concatenate([grad_low, grad_bmat, grad_cmat], axis=1).astype(jnp.bfloat16), "mp"
+        ),
+        axis=0,
     )
     grad_from_proj = lax.dot_general(
         grad_proj, rows_proj, (((1,), (1,)), ((), ())), preferred_element_type=jnp.float32

time: 1260 us -> 1220 us (0.968)
  waiting for transfers between devices: 547 us -> 508 us
    psum x1 -> x0, waiting for transfers between devices: 57.6 us -> none  [body(): lax.psum(jnp.concatenate([grad_low, grad_bmat, grad_cmat], axis=1).astype...]
    all_gather x0 -> x1, waiting for transfers between devices: none -> 19.3 us  [body(): lax.all_gather(jnp.concatenate([grad_low, grad_bmat, grad_cmat], axis=1)....]
where the time goes in v1:
time: 1220 us; the launch traced here: 1210 us
  waiting for transfers between devices  508 us (42%)
  other arithmetic  306 us (25%)
  blocking collectives  281 us (23%)
  local copies, waits for them, and re-layouts  75.5 us (6%)
  between operations  16.1 us (1%)
    unnamed x1, blocking collectives  281 us
    all_gather x3, waiting for transfers between devices, prefix(): everything = jax.tree.map(lambda part: lax.all_gather(part, axis), x)  255 us
    select_n x128, other arithmetic, step(): return jax.tree.map(lambda a, b: jnp.where(reached, a, b), new, before)  117 us
    all_gather x1, waiting for transfers between devices, body(): lax.all_gather(dt_weight, 'ctx', axis=0, tiled=True)  85.5 us
    reduce_sum x8, other arithmetic, block_closed(): gaps = jnp.where(lower, cumul[:, None] - cumul[None, :], 0.0)  85.3 us
    all_gather x1, waiting for transfers between devices, body(): lax.all_gather(proj_weight, 'ctx', axis=0, tiled=True)  81.7 us
    psum x1, waiting for transfers between devices, body(): projected = lax.psum(partial_proj, 'mp')  63.4 us
    reduce_sum x8, other arithmetic, block_closed(): jnp.sum(weights * inflow[None], axis=1)  45.4 us
  transfers between devices with their start and end apart: 10, of which 8 were waited for; matrix products, arithmetic and copies ran while one was open for 2% of the time, Pallas kernels for 0%

profile of v1, /device:TPU:6, one launch (start us, length us, event | category | flops | bytes accessed | tf_op | source)
XLA Modules:
  0.0 1206.9 jit_solution(17664871756566632417)
XLA Ops:
  8.7 3.5 collective-permute-start
  13.8 2.7 multiply_reduce_fusion.15
  16.4 81.7 %all-gather.10.cloned.1.call-done = bf16[1024,544]{1,0:T(8,128)(2,1)} async-done(((bf16[16,544]{1,0:T(8,128)(2,1)}), bf16[1024,544]{1,0:T(8,128)(2,1)}) %all-gather.10.cloned.1.call-update) | async-done | bytes 1114128 | tf_op jit(solution)/shard_map/all_gather | solution.py:108
  98.2 2.7 fusion.83
  101.8 63.4 %all-reduce.14.cloned.1.call-done = f32[128,544]{0,1:T(8,128)} async-done(((f32[128,544]{0,1:T(8,128)}), f32[128,544]{0,1:T(8,128)}) %all-reduce.14.cloned.1.call-update) | async-done | bytes 278544 | tf_op jit(solution)/shard_map/psum | solution.py:112
  167.4 85.5 %all-gather.12.cloned.1.call-done = bf16[512,1024]{1,0:T(8,128)(2,1)} async-done(((bf16[8,1024]{1,0:T(8,128)(2,1)}), bf16[512,1024]{1,0:T(8,128)(2,1)}) %all-gather.12.cloned.1.call-update) | async-done | bytes 1048592 | tf_op jit(solution)/shard_map/all_gather | solution.py:109
  252.9 2.7 compare_select_fusion
  256.4 59.0 %while.128 = (s32[]{:T(128)}, f32[16,1024]{1,0:T(8,128)S(1)}, f32[8,16,1024]{2,1,0:T(8,128)S(1)}, f32[8,16,1024]{2,1,0:T(8,128)S(1)}, f32[8,16,1024]{2,1,0:T(8,1...) while((s32[]{:T(128)}, f32[16,1024]{1,0:T(8,128)S(1)}, ...), condition=%wide.region_6.7_spmd.clone.clone, body=%wide.region_2.6_spmd.clone.clone.sunk | while | flops 26214400 | bytes 9574793 | solution.py:57
  257.6 5.7 multiply_reduce_fusion.25
  265.0 5.7 multiply_reduce_fusion.25
  272.4 5.7 multiply_reduce_fusion.25
  279.8 5.7 multiply_reduce_fusion.25
  287.1 5.7 multiply_reduce_fusion.25
  294.5 5.7 multiply_reduce_fusion.25
  301.9 5.7 multiply_reduce_fusion.25
  309.2 5.7 multiply_reduce_fusion.25
  316.7 83.6 %all-gather.18.cloned.1.call-done = f32[1024,1024]{1,0:T(8,128)} async-done(((f32[16,1024]{1,0:T(8,128)}), f32[1024,1024]{1,0:T(8,128)}) %all-gather.18.cloned.1.call-update) | async-done | bytes 4194320 | tf_op jit(solution)/shard_map/all_gather | solution.py:19
  400.3 87.8 %all-gather.16.cloned.1.call-done = f32[1024,1024]{1,0:T(8,128)} async-done(((f32[16,1024]{1,0:T(8,128)}), f32[1024,1024]{1,0:T(8,128)}) %all-gather.16.cloned.1.call-update) | async-done | bytes 4194320 | tf_op jit(solution)/shard_map/all_gather | solution.py:19
  488.1 59.9 %while.129 = (s32[]{:T(128)}, f32[16,1024]{1,0:T(8,128)S(1)}, s32[]{:T(128)}, f32[64,16,1024]{2,1,0:T(8,128)}, f32[64,16,1024]{2,1,0:T(8,128)}, /*index=5*/s32[]{:T(128)}, s32[]{:T(128)}) while((s32[]{:T(128)}, f32[16,1024]{1,0:T(8,128)S(1)}, s32[]{:T(128)}, f32[64,16,1024]{2,1,0:T(8,128)}, f32[64,16,1024]{2,1,0:T(8,128)}, ...), condition=%wide.region_8.9_spmd.clone, body=%wide.region_7.8_spmd.clone.sunk | while | flops 65540 | bytes 262245 | solution.py:30
  549.1 14.5 %while.126 = (s32[]{:T(128)}, f32[16,1024]{1,0:T(8,128)S(1)}, f32[8,16,1024]{2,1,0:T(8,128)S(1)}, f32[8,16,1024]{2,1,0:T(8,128)}, f32[8,16,1024]{2,1,0:T(8,128)S...) while((s32[]{:T(128)}, f32[16,1024]{1,0:T(8,128)S(1)}, ...), condition=%wide.region_12.13_spmd, body=%wide.region_9.12_spmd.sunk | while | flops 4964354 | bytes 1969769 | solution.py:76
  563.6 8.2 while.127
  573.4 83.1 %all-gather.20.cloned.1.call-done = f32[1024,1024]{1,0:T(8,128)} async-done(((f32[16,1024]{1,0:T(8,128)}), f32[1024,1024]{1,0:T(8,128)}) %all-gather.20.cloned.1.call-update) | async-done | bytes 4194320 | tf_op jit(solution)/shard_map/all_gather | solution.py:19
  656.5 60.4 %while.130 = (s32[]{:T(128)}, f32[16,1024]{1,0:T(8,128)S(1)}, s32[]{:T(128)}, f32[64,16,1024]{2,1,0:T(8,128)}, f32[64,16,1024]{2,1,0:T(8,128)}, /*index=5*/s32[]{:T(128)}, s32[]{:T(128)}, s32[]{:T(128)}, s32[]{:T(128)}) while((s32[]{:T(128)}, f32[16,1024]{1,0:T(8,128)S(1)}, s32[]{:T(128)}, f32[64,16,1024]{2,1,0:T(8,128)}, ...), condition=%wide.region_18.19_spmd.clone, body=%wide.region_17.18_spmd.clone.sunk | while | flops 65544 | bytes 262307 | solution.py:30
  659.3 0.9 fusion.104
  660.2 0.9 fusion.104
  663.1 0.9 fusion.104
  664.0 0.9 fusion.104
  665.0 0.9 fusion.104
  667.8 0.9 fusion.104
  668.7 0.9 fusion.104
  716.9 22.7 %while.132 = (s32[]{:T(128)}, f32[16,1024]{1,0:T(8,128)S(1)}, f32[16,1024]{1,0:T(8,128)S(1)}, f32[8,16,1024]{2,1,0:T(8,128)S(1)}, f32[8,16,16]{2,1,0:T(8,128)S(1...) while((s32[]{:T(128)}, f32[16,1024]{1,0:T(8,128)S(1)}, ...), condition=%wide.region_40.41_spmd.clone, body=%wide.region_33.40_spmd.clone.sunk | while | flops 12041988 | bytes 4084903 | solution.py:76
  739.6 0.9 broadcast.80.clone.6
  741.4 133.5 %while.131 = (s32[]{:T(128)}, f32[16,1024]{1,0:T(8,128)S(1)}, f32[16,1024]{1,0:T(8,128)S(1)}, f32[8,16,1024]{2,1,0:T(8,128)}, f32[8,16,1024]{2,1,0:T(8,128)}, /*...) while((s32[]{:T(128)}, f32[16,1024]{1,0:T(8,128)S(1)}, ...), condition=%wide.region_32.33_spmd.clone, body=%wide.region_19.32_spmd.clone.sunk | while | flops 68452096 | bytes 19693264 | solution.py:57
  741.4 0.9 dynamic-slice_bitcast_fusion.43
  744.6 10.7 fusion.107
  755.6 0.9 multiply_reduce_fusion.28
  761.3 10.7 fusion.107
  772.3 0.9 multiply_reduce_fusion.28
  778.0 10.7 fusion.107
  789.0 0.9 multiply_reduce_fusion.28
  794.7 10.7 fusion.107
  805.6 0.9 multiply_reduce_fusion.28
  811.4 10.7 fusion.107
  822.3 0.9 multiply_reduce_fusion.28
  828.0 10.7 fusion.107
  839.0 0.9 multiply_reduce_fusion.28
  844.7 10.7 fusion.107
  855.7 0.9 multiply_reduce_fusion.28
  861.4 10.7 fusion.107
  872.4 0.9 multiply_reduce_fusion.28
  875.0 1.3 add.255
  876.3 1.9 fusion.79
  880.3 1.7 fusion.74
  882.2 2.6 fusion.69
  884.8 19.3 %all-gather.14.cloned.1.call-done = bf16[8,128,544]{1,2,0:T(8,128)(2,1)} async-done(((bf16[1,128,544]{1,2,0:T(8,128)(2,1)}), bf16[8,128,544]{1,2,0:T(8,128)(2,1)}) %all-gather.14.cloned.1.call-update) | async-done | bytes 1114128 | tf_op jit(solution)/shard_map/all_gather | solution.py:159
  904.1 1.4 reduce_sum.403
  905.6 1.8 fusion.44
  907.4 1.3 collective-permute-start.1
  908.7 1.3 dynamic-slice
  911.3 1.8 collective-permute-done.1
  913.0 1.2 fusion.58
  914.3 280.6 %all-reduce.9 = (f32[4,1024]{1,0:T(4,128)S(1)}, f32[1024]{0:T(1024)S(1)}, f32[1024]{0:T(1024)S(1)}, f32[1024]{0:T(1024)S(1)}) all-reduce(f32[4,1024]{1,0:T(4,128)S(1)} %pad_maximum_fusion.3, f32[1024]{0:T(1024)S(1)} %get-tuple-element.1448, f32[1024]{0:T(1024)S(1)} %copy-done.27, ...), channel_id=6, replica_groups=mesh['ctx'=64,'mp'=8] {'ctx'}, use_global_device_ids=true, to_apply=%region_47.48.clone | all-reduce | flops 7168 | bytes 57344
  1197.3 1.4 constant_dynamic-slice_fusion
  1198.7 1.4 constant_dynamic-slice_fusion.2
  (614 shorter events, 223.1 us)
Async XLA Ops:
  7.2 245.7 %copy-start.28 = (f32[1024]{0:T(1024)S(1)}, f32[1024]{0:T(1024)}, u32[]{:S(2)}) copy-start(f32[1024]{0:T(1024)} %param.33) | copy-start | bytes 12292
  7.2 248.4 %copy-start.13 = (f32[16,1024]{1,0:T(8,128)S(1)}, f32[16,1024]{1,0:T(8,128)}, u32[]{:S(2)}) copy-start(f32[16,1024]{1,0:T(8,128)} %param.34) | copy-start | bytes 196612
  7.2 91.0 %all-gather.10.cloned.1.call-start = ((), (), s32[]{:S(2)}) async-start(), calls=%async_computation | async-start | bytes 1331200 | tf_op jit(solution)/shard_map/all_gather | solution.py:108
  7.9 157.3 %all-reduce.14.cloned.1.call-start = ((), (), s32[]{:S(2)}) async-start(), calls=%async_computation.1 | async-start | bytes 557056 | tf_op jit(solution)/shard_map/psum | solution.py:112
  8.7 5.1 collective-permute-start
  13.1 88.6 %copy-start.16 = (f32[1,1024]{1,0:T(1,128)}, f32[1,1024]{1,0:T(1,128)S(1)}, u32[]{:S(2)}) copy-start(f32[1,1024]{1,0:T(1,128)S(1)} %get-tuple-element.1610) | copy-start | bytes 12292
  13.1 88.6 %copy-start.18 = (f32[1,1024]{1,0:T(1,128)}, f32[1,1024]{1,0:T(1,128)S(1)}, u32[]{:S(2)}) copy-start(f32[1,1024]{1,0:T(1,128)S(1)} %get-tuple-element.1611) | copy-start | bytes 12292
  13.1 88.6 %copy-start.20 = (f32[1,1024]{1,0:T(1,128)}, f32[1,1024]{1,0:T(1,128)S(1)}, u32[]{:S(2)}) copy-start(f32[1,1024]{1,0:T(1,128)S(1)} %get-tuple-element.1612) | copy-start | bytes 12292
  13.1 88.6 %copy-start.22 = (f32[1,1024]{1,0:T(1,128)}, f32[1,1024]{1,0:T(1,128)S(1)}, u32[]{:S(2)}) copy-start(f32[1,1024]{1,0:T(1,128)S(1)} %get-tuple-element.1613) | copy-start | bytes 12292
  13.8 241.8 %copy-start.30 = (f32[128]{0:T(128)}, f32[128]{0:T(128)S(1)}, u32[]{:S(2)}) copy-start(f32[128]{0:T(128)S(1)} %convert_negate_fusion.1) | copy-start | bytes 1540
  13.8 87.9 %copy-start.24 = (bf16[3,1024]{1,0:T(4,128)(2,1)}, bf16[3,1024]{1,0:T(4,128)(2,1)S(1)}, u32[]{:S(2)}) copy-start(bf16[3,1024]{1,0:T(4,128)(2,1)S(1)} %collective-permute-done) | copy-start | bytes 18436
  100.9 152.0 %all-gather.12.cloned.1.call-start = ((), (), s32[]{:S(2)}) async-start(), calls=%async_computation.2 | async-start | bytes 1064960 | tf_op jit(solution)/shard_map/all_gather | solution.py:109
  101.6 298.7 %all-gather.18.cloned.1.call-start = ((), (), s32[]{:S(2)}) async-start(), calls=%async_computation.5 | async-start | bytes 4259840 | tf_op jit(solution)/shard_map/all_gather | solution.py:19
  315.4 0.6 copy-start
  315.4 232.7 %copy-start.7 = (f32[8,16,1024]{2,1,0:T(8,128)}, f32[8,16,1024]{2,1,0:T(8,128)S(1)}, u32[]{:S(2)}) copy-start(f32[8,16,1024]{2,1,0:T(8,128)S(1)} %get-tuple-element.2242) | copy-start | bytes 1572868
  315.4 232.7 %copy-start.8 = (f32[8,16,1024]{2,1,0:T(8,128)}, f32[8,16,1024]{2,1,0:T(8,128)S(1)}, u32[]{:S(2)}) copy-start(f32[8,16,1024]{2,1,0:T(8,128)S(1)} %get-tuple-element.2243) | copy-start | bytes 1572868
  315.4 232.7 %copy-start.4 = (f32[8,16,1024]{2,1,0:T(8,128)}, f32[8,16,1024]{2,1,0:T(8,128)S(1)}, u32[]{:S(2)}) copy-start(f32[8,16,1024]{2,1,0:T(8,128)S(1)} %get-tuple-element.1049) | copy-start | bytes 1572868
  316.0 172.1 %all-gather.16.cloned.1.call-start = ((), (), s32[]{:S(2)}) async-start(), calls=%async_computation.4 | async-start | bytes 4259840 | tf_op jit(solution)/shard_map/all_gather | solution.py:19
  316.6 339.8 %all-gather.20.cloned.1.call-start = ((), (), s32[]{:S(2)}) async-start(), calls=%async_computation.6 | async-start | bytes 4259840 | tf_op jit(solution)/shard_map/all_gather | solution.py:19
  563.6 153.3 %copy-start.5 = (f32[8,16,1024]{2,1,0:T(8,128)}, f32[8,16,1024]{2,1,0:T(8,128)S(1)}, u32[]{:S(2)}) copy-start(f32[8,16,1024]{2,1,0:T(8,128)S(1)} %get-tuple-element.1050) | copy-start | bytes 1572868
  571.8 0.6 copy-start.2
  572.5 331.6 %all-gather.14.cloned.1.call-start = ((), (), s32[]{:S(2)}) async-start(), calls=%async_computation.3 | async-start | bytes 1253376 | tf_op jit(solution)/shard_map/all_gather | solution.py:159
  739.6 1.8 copy-start.6
  741.4 136.8 %copy-start.1 = (bf16[512,1024]{1,0:T(8,128)(2,1)S(1)}, bf16[512,1024]{1,0:T(8,128)(2,1)}, u32[]{:S(2)}) copy-start(bf16[512,1024]{1,0:T(8,128)(2,1)} %all-gather.12.cloned.1.call-done) | copy-start | bytes 3145732
  875.0 3.8 copy-start.15
  875.0 4.7 copy-start.14
  875.0 5.3 copy-start.11
  876.3 5.8 copy-start.3
  876.3 5.8 copy-start.12
  879.6 317.7 %all-reduce.16.cloned.1.call-start = ((), (), s32[]{:S(2)}) async-start(), calls=%async_computation.7 | async-start | bytes 4325376
  882.1 23.5 %copy-start.9 = (bf16[1024,544]{1,0:T(8,128)(2,1)S(1)}, bf16[1024,544]{1,0:T(8,128)(2,1)}, u32[]{:S(2)}) copy-start(bf16[1024,544]{1,0:T(8,128)(2,1)} %all-gather.10.cloned.1.call-done) | copy-start | bytes 3342340
  882.1 23.5 %copy-start.10 = (bf16[128,1024]{1,0:T(8,128)(2,1)S(1)}, bf16[128,1024]{1,0:T(8,128)(2,1)}, u32[]{:S(2)}) copy-start(bf16[128,1024]{1,0:T(8,128)(2,1)} %param.25) | copy-start | bytes 786436
  882.1 23.5 %copy-start.17 = (f32[1,1024]{1,0:T(1,128)S(1)}, f32[1,1024]{1,0:T(1,128)}, u32[]{:S(2)}) copy-start(f32[1,1024]{1,0:T(1,128)} %copy-done.16) | copy-start | bytes 12292
  882.1 23.5 %copy-start.19 = (f32[1,1024]{1,0:T(1,128)S(1)}, f32[1,1024]{1,0:T(1,128)}, u32[]{:S(2)}) copy-start(f32[1,1024]{1,0:T(1,128)} %copy-done.18) | copy-start | bytes 12292
  882.1 23.5 %copy-start.21 = (f32[1,1024]{1,0:T(1,128)S(1)}, f32[1,1024]{1,0:T(1,128)}, u32[]{:S(2)}) copy-start(f32[1,1024]{1,0:T(1,128)} %copy-done.20) | copy-start | bytes 12292
  882.1 23.5 %copy-start.23 = (f32[1,1024]{1,0:T(1,128)S(1)}, f32[1,1024]{1,0:T(1,128)}, u32[]{:S(2)}) copy-start(f32[1,1024]{1,0:T(1,128)} %copy-done.22) | copy-start | bytes 12292
  882.1 23.5 %copy-start.25 = (bf16[3,1024]{1,0:T(4,128)(2,1)S(1)}, bf16[3,1024]{1,0:T(4,128)(2,1)}, u32[]{:S(2)}) copy-start(bf16[3,1024]{1,0:T(4,128)(2,1)} %copy-done.24) | copy-start | bytes 18436
  882.1 23.5 %copy-start.29 = (f32[1024]{0:T(1024)S(1)}, f32[1024]{0:T(1024)}, u32[]{:S(2)}) copy-start(f32[1024]{0:T(1024)} %param.30) | copy-start | bytes 12292
  905.5 8.8 copy-start.26
  905.5 8.8 copy-start.27
  907.4 5.6 collective-permute-start.1
Sparse Core Ops, SparseCore 0:
  11.1 87.0 all-gather.9
  101.0 64.1 all-reduce.13
  168.7 84.1 all-gather.11
  316.2 84.1 all-gather.17
  404.3 83.8 all-gather.15
  572.6 83.8 all-gather.19
  879.8 24.2 all-gather.13
  907.9 164.9 all-reduce.15
